TPU v7x, 32 devices: a whole 2x2x4 slice. The times are simulated.
32 devices in a mesh: dp: 4 (over z), expert: 8 (over y, x, core).
Axes of the slice: x: 2, y: 2, z: 4, core: 2. Of those that a mesh axis runs over, the one named last changes fastest.
Arguments:
- block_input: bfloat16 [12608, 768], P(('dp', 'expert')), may hold values from -6 to 6
- out_grad: bfloat16 [12608, 768], P(('dp', 'expert')), may hold values from -6 to 6
- expert_ids: int32 [12608, 2], P(('dp', 'expert')), may hold values from 0 to 7, all different within a row
- slot_order: int32 [32, 394], P(('dp', 'expert')), may hold values from 0 to 393, each once within a row
- joint_weight: bfloat16 [768, 2304], P('expert'), may hold values from -0.21875 to 0.21875
- out_weight: bfloat16 [768, 768], P('expert'), may hold values from -0.625 to 0.625
- router_weight: bfloat16 [768, 8], P('expert'), may hold values from -0.4375 to 0.4375
- norm_gains: bfloat16 [2, 768], P(None, 'expert'), may hold values from 0.099609375 to 1.8984375
- norm_shifts: bfloat16 [2, 768], P(None, 'expert'), may hold values from -3 to 3
- attention_bias: bfloat16 [3, 768], P(None, 'expert'), may hold values from -3 to 3
- up_weight: bfloat16 [8, 768, 3072], P('expert'), may hold values from -0.21875 to 0.21875
- down_weight: bfloat16 [8, 3072, 768], P('expert'), may hold values from -3.5 to 3.5
- up_bias: bfloat16 [8, 3072], P('expert'), may hold values from -3 to 3
- down_bias: bfloat16 [8, 768], P('expert'), may hold values from -4 to 4
Outputs:
- block_output: bfloat16 [12608, 768], P(('dp', 'expert'))
- input_grad: bfloat16 [12608, 768], P(('dp', 'expert'))
- joint_grad: float32 [768, 2304], P('expert')
- out_weight_grad: float32 [768, 768], P('expert')
- router_grad: float32 [768, 8], P('expert')
- gains_grad: float32 [2, 768], P(None, 'expert')
- shifts_grad: float32 [2, 768], P(None, 'expert')
- attention_bias_grad: float32 [3, 768], P(None, 'expert')
- up_grad: float32 [8, 768, 3072], P('expert', None, 'dp')
- down_grad: float32 [8, 3072, 768], P('expert', 'dp')
- up_bias_grad: float32 [8, 3072], P('expert', 'dp')
- down_bias_grad: float32 [8, 768], P('expert', 'dp')
Inputs may be any that keep to these rules, and one draw needn't show every extreme that they name: `expert_ids`: the two experts of a token differ. `slot_order`: each row is a permutation of the 394 token positions of one device.
All inputs are finite; a program needn't handle non-finite values.
Results may differ from a plain program's by a relative error of at most 0.024.
Values may be sent and summed in bfloat16 or wider, within the bound.
No kernel may reach another device: no remote copies, remote signals or barrier semaphores. Data moves between devices by JAX's collectives and lax.ppermute only.
A program may use at most 192 MiB of HBM per device.

v0:
```python
import jax
import jax.numpy as jnp
from jax import lax
from jax.sharding import PartitionSpec as P

HEADS = 12
HEAD_DIM = 64
SEQ = 197
norm_eps = 1e-06


def layer_norm(values, gain_row, shift_row):
    row_mean = jnp.mean(values, axis=-1, keepdims=True)
    centered = values - row_mean
    row_var = jnp.mean(centered * centered, axis=-1, keepdims=True)
    return centered * lax.rsqrt(row_var + norm_eps) * gain_row + shift_row


def gelu_tanh(values):
    return jax.nn.gelu(values, approximate=True)


def slot_table(route_rows, order_row, expert_count, capacity):
    tokens_here = route_rows.shape[0]
    ordered = jnp.take(route_rows, order_row, axis=0)
    expert_iota = jnp.arange(expert_count, dtype=jnp.int32)
    first_hot = (ordered[:, 0:1] == expert_iota[None, :]).astype(jnp.int32)
    second_hot = (ordered[:, 1:2] == expert_iota[None, :]).astype(jnp.int32)
    first_slot = jnp.sum((jnp.cumsum(first_hot, axis=0) - first_hot) * first_hot, axis=1)
    second_base = jnp.sum(first_hot, axis=0, keepdims=True)
    second_slot = jnp.sum(
        (jnp.cumsum(second_hot, axis=0) - second_hot + second_base) * second_hot, axis=1
    )
    slot_rank = jnp.stack([first_slot, second_slot], axis=1)
    flat_rank = jnp.where(
        slot_rank < capacity, ordered * capacity + slot_rank, expert_count * capacity
    )
    token_flat = jnp.zeros((tokens_here, 2), jnp.int32).at[order_row].set(flat_rank)
    token_index = jnp.broadcast_to(
        jnp.arange(tokens_here, dtype=jnp.int32)[:, None], (tokens_here, 2)
    )
    source = (
        jnp.full((expert_count * capacity,), tokens_here, jnp.int32)
        .at[token_flat.reshape(-1)]
        .set(token_index.reshape(-1), mode="drop")
    )
    return (token_flat, source)


def per_device(
    block_input,
    out_grad,
    expert_ids,
    slot_order,
    joint_weight,
    out_weight,
    router_weight,
    norm_gains,
    norm_shifts,
    attention_bias,
    up_weight,
    down_weight,
    up_bias,
    down_bias,
):
    joint_full, out_full, router_full, gains_low, shifts_low, bias_low = (
        lax.all_gather(joint_weight, "expert", axis=0, tiled=True),
        lax.all_gather(out_weight, "expert", axis=0, tiled=True),
        lax.all_gather(router_weight, "expert", axis=0, tiled=True),
        lax.all_gather(norm_gains, "expert", axis=1, tiled=True),
        lax.all_gather(norm_shifts, "expert", axis=1, tiled=True),
        lax.all_gather(attention_bias, "expert", axis=1, tiled=True),
    )
    gains = gains_low.astype(jnp.float32)
    shifts = shifts_low.astype(jnp.float32)
    biases = bias_low.astype(jnp.float32)
    row_count, features = block_input.shape
    images = row_count // SEQ
    experts = router_full.shape[1]
    local_experts = up_weight.shape[0]
    capacity = max(2, (5 * row_count + 2 * experts - 1) // (2 * experts))
    head_scale = HEAD_DIM ** (-0.5)
    input_float = block_input.astype(jnp.float32)
    normed, norm_back = jax.vjp(layer_norm, input_float, gains[0], shifts[0])
    normed_low = normed.astype(jnp.bfloat16)
    joint_bias = jnp.concatenate([biases[0], jnp.zeros_like(biases[0]), biases[1]])
    projected = (
        jnp.dot(normed_low, joint_full, preferred_element_type=jnp.float32) + joint_bias
    ).astype(jnp.bfloat16)
    projected = projected.reshape(images, SEQ, 3, HEADS, HEAD_DIM)
    query_heads = projected[:, :, 0]
    key_heads = projected[:, :, 1]
    value_heads = projected[:, :, 2]
    scores = (
        jnp.einsum("ishd,ithd->ihst", query_heads, key_heads, preferred_element_type=jnp.float32)
        * head_scale
    )
    score_max = jnp.max(scores, axis=-1, keepdims=True)
    shifted = jnp.exp(scores - score_max)
    score_total = jnp.sum(shifted, axis=-1, keepdims=True)
    weighting = shifted / score_total
    log_total = score_max + jnp.log(score_total)
    attended = jnp.einsum(
        "ihst,ithd->ishd",
        weighting.astype(jnp.bfloat16),
        value_heads,
        preferred_element_type=jnp.float32,
    )
    attended_low = attended.reshape(row_count, features).astype(jnp.bfloat16)
    residual = (
        input_float
        + jnp.dot(attended_low, out_full, preferred_element_type=jnp.float32)
        + biases[2]
    )
    normed_two, norm_two_back = jax.vjp(layer_norm, residual, gains[1], shifts[1])
    two_low = normed_two.astype(jnp.bfloat16)
    logits = jnp.dot(two_low, router_full, preferred_element_type=jnp.float32)
    gate_weights = jax.nn.softmax(logits, axis=-1)
    chosen = jnp.take_along_axis(gate_weights, expert_ids, axis=1)
    token_flat, source = slot_table(expert_ids, slot_order[0], experts, capacity)
    dispatched = jnp.take(two_low, source, axis=0, mode="fill", fill_value=0).reshape(
        experts, capacity, features
    )
    arrived = lax.all_to_all(dispatched, "expert", split_axis=0, concat_axis=0, tiled=True)
    arrived_rows = arrived.reshape(-1, local_experts, capacity, features)
    pre_gelu = (
        jnp.einsum("secd,edf->secf", arrived_rows, up_weight, preferred_element_type=jnp.float32)
        + up_bias.astype(jnp.float32)[None, :, None, :]
    )
    hidden, gelu_back = jax.vjp(gelu_tanh, pre_gelu)
    hidden_low = hidden.astype(jnp.bfloat16)
    expert_out = (
        jnp.einsum("secf,efd->secd", hidden_low, down_weight, preferred_element_type=jnp.float32)
        + down_bias.astype(jnp.float32)[None, :, None, :]
    )
    expert_low = expert_out.astype(jnp.bfloat16).reshape(-1, capacity, features)
    returned = lax.all_to_all(
        expert_low, "expert", split_axis=0, concat_axis=0, tiled=True
    ).reshape(experts * capacity, features)
    picked = jnp.take(returned, token_flat, axis=0, mode="fill", fill_value=0).astype(jnp.float32)
    block_output = (residual + jnp.sum(chosen[:, :, None] * picked, axis=1)).astype(jnp.bfloat16)
    grad_float = out_grad.astype(jnp.float32)
    gate_grad = jnp.sum(grad_float[:, None, :] * picked, axis=2)
    pair_grad = (chosen[:, :, None] * grad_float[:, None, :]).astype(jnp.bfloat16)
    slot_grad = (
        jnp.zeros((experts * capacity, features), jnp.bfloat16)
        .at[token_flat.reshape(-1)]
        .set(pair_grad.reshape(-1, features), mode="drop")
    )
    grad_arrived = lax.all_to_all(
        slot_grad.reshape(experts, capacity, features),
        "expert",
        split_axis=0,
        concat_axis=0,
        tiled=True,
    )
    grad_rows = grad_arrived.reshape(-1, local_experts, capacity, features)
    hidden_grad = jnp.einsum(
        "secd,efd->secf", grad_rows, down_weight, preferred_element_type=jnp.float32
    )
    (inner_grad,) = gelu_back(hidden_grad)
    inner_low = inner_grad.astype(jnp.bfloat16)
    rows_grad = jnp.einsum(
        "secf,edf->secd", inner_low, up_weight, preferred_element_type=jnp.float32
    ).astype(jnp.bfloat16)
    rows_back = lax.all_to_all(
        rows_grad.reshape(-1, capacity, features), "expert", split_axis=0, concat_axis=0, tiled=True
    ).reshape(experts * capacity, features)
    up_local = jnp.einsum(
        "secd,secf->edf", arrived_rows, inner_low, preferred_element_type=jnp.float32
    )
    down_local = jnp.einsum(
        "secf,secd->efd", hidden_low, grad_rows, preferred_element_type=jnp.float32
    )
    up_bias_local = jnp.sum(inner_low, axis=(0, 2), dtype=jnp.float32)
    down_bias_local = jnp.sum(grad_rows, axis=(0, 2), dtype=jnp.float32)
    up_grad, down_grad, up_bias_grad, down_bias_grad = (
        lax.psum_scatter(
            up_local.astype(jnp.bfloat16), "dp", scatter_dimension=2, tiled=True
        ).astype(jnp.float32),
        lax.psum_scatter(
            down_local.astype(jnp.bfloat16), "dp", scatter_dimension=1, tiled=True
        ).astype(jnp.float32),
        lax.psum_scatter(
            up_bias_local.astype(jnp.bfloat16), "dp", scatter_dimension=1, tiled=True
        ).astype(jnp.float32),
        lax.psum_scatter(
            down_bias_local.astype(jnp.bfloat16), "dp", scatter_dimension=1, tiled=True
        ).astype(jnp.float32),
    )
    joint_back, out_back, router_back = (
        lax.all_gather(joint_weight, "expert", axis=0, tiled=True),
        lax.all_gather(out_weight, "expert", axis=0, tiled=True),
        lax.all_gather(router_weight, "expert", axis=0, tiled=True),
    )
    expert_iota = jnp.arange(experts, dtype=jnp.int32)
    choice_hot = (expert_ids[:, :, None] == expert_iota[None, None, :]).astype(jnp.float32)
    mass_grad = jnp.sum(gate_grad[:, :, None] * choice_hot, axis=1)
    logit_grad = (
        gate_weights * (mass_grad - jnp.sum(gate_weights * mass_grad, axis=1, keepdims=True))
    ).astype(jnp.bfloat16)
    router_local = jnp.einsum("td,te->de", two_low, logit_grad, preferred_element_type=jnp.float32)
    two_grad = jnp.einsum("te,de->td", logit_grad, router_back, preferred_element_type=jnp.float32)
    two_grad = two_grad + jnp.sum(
        jnp.take(rows_back, token_flat, axis=0, mode="fill", fill_value=0).astype(jnp.float32),
        axis=1,
    )
    residual_part, gain_two, shift_two = norm_two_back(two_grad)
    residual_grad = grad_float + residual_part
    branch_low = residual_grad.astype(jnp.bfloat16)
    out_local = jnp.einsum(
        "td,te->de", attended_low, branch_low, preferred_element_type=jnp.float32
    )
    attended_grad = jnp.einsum(
        "te,de->td", branch_low, out_back, preferred_element_type=jnp.float32
    )
    attended_grad = attended_grad.astype(jnp.bfloat16).reshape(images, SEQ, HEADS, HEAD_DIM)
    scores_again = (
        jnp.einsum("ishd,ithd->ihst", query_heads, key_heads, preferred_element_type=jnp.float32)
        * head_scale
    )
    weighting_again = jnp.exp(scores_again - log_total)
    weight_grad = jnp.einsum(
        "ishd,ithd->ihst", attended_grad, value_heads, preferred_element_type=jnp.float32
    )
    value_grad = jnp.einsum(
        "ihst,ishd->ithd",
        weighting_again.astype(jnp.bfloat16),
        attended_grad,
        preferred_element_type=jnp.float32,
    )
    score_grad = (
        weighting_again
        * (weight_grad - jnp.sum(weight_grad * weighting_again, axis=-1, keepdims=True))
    ).astype(jnp.bfloat16)
    query_grad = (
        jnp.einsum("ihst,ithd->ishd", score_grad, key_heads, preferred_element_type=jnp.float32)
        * head_scale
    )
    key_grad = (
        jnp.einsum("ihst,ishd->ithd", score_grad, query_heads, preferred_element_type=jnp.float32)
        * head_scale
    )
    projected_grad = (
        jnp.stack([query_grad, key_grad, value_grad], axis=2)
        .reshape(row_count, 3 * features)
        .astype(jnp.bfloat16)
    )
    joint_local = jnp.einsum(
        "td,te->de", normed_low, projected_grad, preferred_element_type=jnp.float32
    )
    bias_sums = jnp.sum(projected_grad, axis=0, dtype=jnp.float32)
    normed_grad = jnp.einsum(
        "te,de->td", projected_grad, joint_back, preferred_element_type=jnp.float32
    )
    input_part, gain_one, shift_one = norm_back(normed_grad)
    input_grad = (residual_grad + input_part).astype(jnp.bfloat16)
    gains_local = jnp.stack([gain_one, gain_two])
    shifts_local = jnp.stack([shift_one, shift_two])
    bias_local = jnp.stack(
        [bias_sums[:features], bias_sums[2 * features :], jnp.sum(residual_grad, axis=0)]
    )
    joint_part, out_part, router_part, gains_part, shifts_part, bias_part = (
        lax.psum_scatter(
            joint_local.astype(jnp.bfloat16), "expert", scatter_dimension=0, tiled=True
        ).astype(jnp.float32),
        lax.psum_scatter(
            out_local.astype(jnp.bfloat16), "expert", scatter_dimension=0, tiled=True
        ).astype(jnp.float32),
        lax.psum_scatter(
            router_local.astype(jnp.bfloat16), "expert", scatter_dimension=0, tiled=True
        ).astype(jnp.float32),
        lax.psum_scatter(
            gains_local.astype(jnp.bfloat16), "expert", scatter_dimension=1, tiled=True
        ).astype(jnp.float32),
        lax.psum_scatter(
            shifts_local.astype(jnp.bfloat16), "expert", scatter_dimension=1, tiled=True
        ).astype(jnp.float32),
        lax.psum_scatter(
            bias_local.astype(jnp.bfloat16), "expert", scatter_dimension=1, tiled=True
        ).astype(jnp.float32),
    )
    joint_grad, out_weight_grad, router_grad, gains_grad, shifts_grad, attention_bias_grad = (
        lax.psum(joint_part.astype(jnp.bfloat16), "dp").astype(jnp.float32),
        lax.psum(out_part.astype(jnp.bfloat16), "dp").astype(jnp.float32),
        lax.psum(router_part.astype(jnp.bfloat16), "dp").astype(jnp.float32),
        lax.psum(gains_part.astype(jnp.bfloat16), "dp").astype(jnp.float32),
        lax.psum(shifts_part.astype(jnp.bfloat16), "dp").astype(jnp.float32),
        lax.psum(bias_part.astype(jnp.bfloat16), "dp").astype(jnp.float32),
    )
    return (
        block_output,
        input_grad,
        joint_grad,
        out_weight_grad,
        router_grad,
        gains_grad,
        shifts_grad,
        attention_bias_grad,
        up_grad,
        down_grad,
        up_bias_grad,
        down_bias_grad,
    )


def solution(mesh):
    in_specs = (
        P(("dp", "expert"), None),
        P(("dp", "expert"), None),
        P(("dp", "expert"), None),
        P(("dp", "expert"), None),
        P("expert", None),
        P("expert", None),
        P("expert", None),
        P(None, "expert"),
        P(None, "expert"),
        P(None, "expert"),
        P("expert", None, None),
        P("expert", None, None),
        P("expert", None),
        P("expert", None),
    )
    out_specs = (
        P(("dp", "expert"), None),
        P(("dp", "expert"), None),
        P("expert", None),
        P("expert", None),
        P("expert", None),
        P(None, "expert"),
        P(None, "expert"),
        P(None, "expert"),
        P("expert", None, "dp"),
        P("expert", "dp", None),
        P("expert", "dp"),
        P("expert", "dp"),
    )
    return jax.shard_map(
        per_device, mesh=mesh, in_specs=in_specs, out_specs=out_specs, check_vma=False
    )
```

profile of v0, /device:TPU:0, one launch (start us, length us, event | category | flops | bytes accessed | tf_op | source)
XLA Modules:
  0.0 785.0 jit_solution(7141210550305157832)
XLA Ops:
  14.9 1.5 scatter_custom_fusion
  16.8 5.3 scatter_custom_fusion.1
  23.2 10.3 %all-gather = bf16[8,96,2]{1,2,0:T(2,128)(2,1)S(1)} all-gather(bf16[1,96,2]{1,2,0:T(2,128)(2,1)S(1)} %bitcast.274), channel_id=1, replica_groups=mesh['dp'=4,'expert'=8] {'expert'}, dimensions={0}, use_global_device_ids=true | all-gather | bytes 3456 | tf_op jit(solution)/shard_map/all_gather | solution.py:70
  33.6 9.2 %all-gather.2 = bf16[8,96,3]{1,2,0:T(4,128)(2,1)S(1)} all-gather(bf16[1,96,3]{1,2,0:T(4,128)(2,1)S(1)} %bitcast.273), channel_id=1, replica_groups=mesh['dp'=4,'expert'=8] {'expert'}, dimensions={0}, use_global_device_ids=true | all-gather | bytes 5184 | tf_op jit(solution)/shard_map/all_gather | solution.py:72
  42.9 7.8 all-gather.1
  51.0 3.7 fusion.36
  54.8 4.9 reshape.440
  59.8 5.0 fusion.123
  64.7 1.6 copy.210
  66.4 2.5 copy.211
  68.9 2.5 copy.209
  77.1 2.3 fusion.126
  80.7 5.2 gather_fusion.1
  85.9 1.5 gather.20
  88.8 4.4 all-to-all-start
  93.3 24.0 %all-gather.3 = bf16[8,96,8]{1,2,0:T(8,128)(2,1)S(1)} all-gather(bf16[1,96,8]{1,2,0:T(8,128)(2,1)S(1)} %bitcast.272), channel_id=1, replica_groups=mesh['dp'=4,'expert'=8] {'expert'}, dimensions={0}, use_global_device_ids=true | all-gather | bytes 13824 | tf_op jit(solution)/shard_map/all_gather | solution.py:69
  117.7 2.1 mul.253
  119.8 3.3 mul.261
  123.5 8.1 %gather_fusion.2 = f32[788]{0:T(1024)S(1)} fusion(f32[394,8]{0,1:T(8,128)S(1)} %fusion.99, s32[788]{0:T(1024)S(1)} %reshape.365), kind=kCustom, calls=%fused_computation.4 | custom fusion | bytes 12608 | tf_op jit(solution)/shard_map/jit(take_along_axis)/gather | solution.py:119
  132.2 8.8 %scatter_custom_fusion.2 = bf16[992,768]{1,0:T(8,128)(2,1)} fusion(s32[788]{0:T(1024)S(1)} %fusion.101, f32[788,768]{1,0:T(8,128)S(1)} %mul.261, f32[788]{0:T(1024)S(1)} %mul.259, bf16[]{:T(256)} %constant.104.clone.1), kind=kCustom, calls=%fused_computation.104 | custom fusion | flops 1210368 | bytes 3960834 | tf_op jit(solution)/shard_map/scatter | solution.py:148
  141.0 2.4 reshape.321
  143.4 3.9 all-to-all-start.2
  147.4 10.0 %fusion.27 = f32[8,124,3072]{2,1,0:T(8,128)} fusion(bf16[8,124,768]{2,1,0:T(8,128)(2,1)} %all-to-all-done, bf16[1,768,3072]{2,1,0:T(8,128)(2,1)} %param.26), kind=kOutput, calls=%fused_computation.46 | convolution fusion | flops 4680843264 | bytes 18432000 | tf_op jit(solution)/shard_map/secd,edf->secf/dot_general | solution.py:127
  157.4 10.9 %all-to-all-done.2 = bf16[8,124,768]{2,1,0:T(8,128)(2,1)S(1)} async-done(((bf16[8,124,768]{2,1,0:T(8,128)(2,1)}), bf16[8,124,768]{2,1,0:T(8,128)(2,1)S(1)}, u32[]{:S(2)}, u32[]{:S(2)}) %all-to-all-start.2) | async-done | bytes 1523744 | tf_op jit(solution)/shard_map/all_to_all | solution.py:150
  168.3 15.5 %fusion.128 = (bf16[3072]{0:T(1024)(128)(2,1)S(1)}, bf16[8,1,124,3072]{3,2,0,1:T(8,128)(2,1)S(1)}) fusion(f32[3072]{0:T(1024)S(1)} %bitcast.264, f32[8,124,3072]{2,1,0:T(8,128)} %fusion.27, bf16[8,124,768]{2,1,0:T(8,128)(2,1)S(1)} %all-to-all-done.2, bf16[1,3072,768]{2,1,0:T(8,128)(2,1)} %param.27), kind=kOutput, calls=%fused_computation.213 | convolution fusion | flops 4747883520 | bytes 24545280 | tf_op jit(solution)/shard_map/secd,efd->secf/dot_general | solution.py:158
  183.8 2.6 copy-done.51
  186.4 8.5 %fusion.56 = bf16[8,124,768]{2,1,0:T(8,128)(2,1)} fusion(bf16[1,768,3072]{2,1,0:T(8,128)(2,1)} %param.26, bf16[8,1,124,3072]{3,2,0,1:T(8,128)(2,1)S(1)} %get-tuple-element.63), kind=kOutput, calls=%fused_computation.78 | convolution fusion | flops 4681605120 | bytes 12337152 | tf_op jit(solution)/shard_map/secf,edf->secd/dot_general | solution.py:163
  194.9 3.6 all-to-all-start.3
  198.5 13.0 %fusion.61 = bf16[8,124,768]{2,1,0:T(8,128)(2,1)} fusion(f32[768]{0:T(1024)S(1)} %convert_reduce_fusion.3, bf16[1,3072,768]{2,1,0:T(8,128)(2,1)} %param.27, f32[8,124,3072]{2,1,0:T(8,128)} %fusion.27, f32[3072]{0:T(1024)S(1)} %bitcast.265), kind=kOutput, calls=%fused_computation.83 | convolution fusion | flops 4712841216 | bytes 18447360 | tf_op jit(solution)/shard_map/secf,efd->secd/dot_general | solution.py:133
  211.5 8.0 %all-to-all-done.3 = bf16[8,124,768]{2,1,0:T(8,128)(2,1)S(1)} async-done(((bf16[8,124,768]{2,1,0:T(8,128)(2,1)}), bf16[8,124,768]{2,1,0:T(8,128)(2,1)S(1)}, u32[]{:S(2)}, u32[]{:S(2)}) %all-to-all-start.3) | async-done | bytes 1523744 | tf_op jit(solution)/shard_map/all_to_all | solution.py:166
  219.5 4.3 all-to-all-start.1
  226.0 3.7 gather_fusion.4
  229.7 1.9 reshape.423
  231.6 13.2 %all-to-all-done.1 = bf16[8,124,768]{2,1,0:T(8,128)(2,1)} async-done(((bf16[8,124,768]{2,1,0:T(8,128)(2,1)}), bf16[8,124,768]{2,1,0:T(8,128)(2,1)}, u32[]{:S(2)}, u32[]{:S(2)}) %all-to-all-start.1) | async-done | bytes 1523744 | tf_op jit(solution)/shard_map/all_to_all | solution.py:137
  244.8 1.5 reshape.320
  246.3 3.7 gather_fusion.3
  250.0 1.9 reshape.419
  251.9 15.9 %fusion.47 = (f32[394,2]{1,0:T(8,128)S(1)}, f32[394,768]{1,0:T(8,128)}, f32[394,768]{1,0:T(8,128)S(1)}) fusion(f32[394,768]{1,0:T(8,128)} %convert_element_type.195, bf16[394,2,768]{2,1,0:T(2,128)(2,1)} %reshape.419, pred[394,2]{1,0:T(8,128)(4,1)S(1)} %compare_and_fusion, f32[394,2]{1,0:T(8,128)S(1)} %copy.171, bf16[394,2,768]{2,1,0:T(2,128)(2,1)} %reshape.423), kind=kLoop, calls=%fused_computation.65 | loop fusion | flops 4840684 | bytes 6058932 | tf_op jit(solution)/shard_map/reduce_sum | solution.py:143
  269.4 1.4 fusion.122
  270.8 1.9 convolution_convert_fusion.1
  272.7 2.0 convolution_convert_fusion.2
  278.0 3.9 multiply_reduce_fusion
  281.9 3.8 multiply_convert_fusion.1
  289.5 3.9 copy.184
  293.4 6.6 convert_element_type.206
  300.0 5.8 convolution_convert_fusion
  310.1 5.0 fusion.120
  316.4 1.5 fusion.119
  322.0 42.4 %reduce-scatter.23.cloned.1.call-done = bf16[96,2304]{1,0:T(8,128)(2,1)} async-done(((bf16[768,2304]{1,0:T(8,128)(2,1)}), bf16[96,2304]{1,0:T(8,128)(2,1)}) %reduce-scatter.23.cloned.1.call-update) | async-done | bytes 442384 | tf_op jit(solution)/shard_map/reduce_scatter | solution.py:264
  364.5 12.2 %fusion.32 = bf16[1,3072,768]{2,1,0:T(8,128)(2,1)} fusion(bf16[8,124,768]{2,1,0:T(8,128)(2,1)S(1)} %copy-done.12, f32[8,124,3072]{2,1,0:T(8,128)} %fusion.27, f32[3072]{0:T(1024)S(1)} %bitcast.266), kind=kOutput, calls=%fused_computation.49 | convolution fusion | flops 4713676800 | bytes 18444288 | tf_op jit(solution)/shard_map/secf,secd->efd/dot_general | solution.py:172
  376.7 9.1 %fusion.29 = bf16[1,768,3072]{2,1,0:T(8,128)(2,1)} fusion(bf16[8,124,768]{2,1,0:T(8,128)(2,1)} %all-to-all-done, bf16[8,1,124,3072]{3,2,0,1:T(8,128)(2,1)} %copy-done.51), kind=kOutput, calls=%fused_computation.48 | convolution fusion | flops 4683202560 | bytes 12337152 | tf_op jit(solution)/shard_map/secd,secf->edf/dot_general | solution.py:169
  387.6 22.7 %reduce-scatter.39.cloned.1.call-done = bf16[768,1]{1,0:T(8,128)(2,1)} async-done(((bf16[3072,1]{1,0:T(8,128)(2,1)}), bf16[768,1]{1,0:T(8,128)(2,1)}) %reduce-scatter.39.cloned.1.call-update) | async-done | bytes 1552
  412.0 35.1 %reduce-scatter.35.cloned.1.call-done = bf16[96,2]{1,0:T(8,128)(2,1)} async-done(((bf16[768,2]{1,0:T(8,128)(2,1)}), bf16[96,2]{1,0:T(8,128)(2,1)}) %reduce-scatter.35.cloned.1.call-update) | async-done | bytes 400
  447.9 36.4 %reduce-scatter.33.cloned.1.call-done = bf16[96,2]{1,0:T(8,128)(2,1)} async-done(((bf16[768,2]{1,0:T(8,128)(2,1)}), bf16[96,2]{1,0:T(8,128)(2,1)}) %reduce-scatter.33.cloned.1.call-update) | async-done | bytes 400
  485.1 35.9 %reduce-scatter.37.cloned.1.call-done = bf16[96,3]{1,0:T(8,128)(2,1)} async-done(((bf16[768,3]{1,0:T(8,128)(2,1)}), bf16[96,3]{1,0:T(8,128)(2,1)}) %reduce-scatter.37.cloned.1.call-update) | async-done | bytes 592
  521.8 36.3 %reduce-scatter.31.cloned.1.call-done = bf16[96,8]{1,0:T(8,128)(2,1)} async-done(((bf16[768,8]{1,0:T(8,128)(2,1)}), bf16[96,8]{1,0:T(8,128)(2,1)}) %reduce-scatter.31.cloned.1.call-update) | async-done | bytes 1552
  558.9 11.7 %all-reduce.2 = (bf16[96,8]{0,1:T(8,128)(2,1)S(1)}, bf16[2,96]{1,0:T(2,128)(2,1)S(1)}, bf16[2,96]{1,0:T(2,128)(2,1)S(1)}, bf16[3,96]{1,0:T(4,128)(2,1)S(1)}) all-reduce(bf16[96,8]{0,1:T(8,128)(2,1)S(1)} %copy.194, bf16[2,96]{1,0:T(2,128)(2,1)S(1)} %copy.196, ...), channel_id=1, replica_groups=mesh['dp'=4,'expert'=8] {'dp'}, use_global_device_ids=true, to_apply=%region_33.35 | all-reduce | flops 1440 | bytes 5760 | tf_op jit(solution)/shard_map/psum | solution.py:286
  572.9 27.4 %all-reduce.6.cloned.1.call-done = (bf16[96,2304]{1,0:T(8,128)(2,1)}, bf16[96,768]{1,0:T(8,128)(2,1)}) async-done(((bf16[96,2304]{1,0:T(8,128)(2,1)}, bf16[96,768]{1,0:T(8,128)(2,1)}), (bf16[96,2304]{1,0:T(8,128)(2,1)}, bf16[96,768]{1,0:T(8,128)(2,1)})) %all-reduce.6.cloned.1.call-update) | async-done | bytes 589840 | tf_op jit(solution)/shard_map/psum | solution.py:284
  600.3 2.0 convert_element_type.209
  602.3 1.6 convert_element_type.211
  603.9 83.3 %reduce-scatter.29.cloned.1.call-done = bf16[1,768,768]{2,1,0:T(8,128)(2,1)} async-done(((bf16[1,3072,768]{2,1,0:T(8,128)(2,1)}), bf16[1,768,768]{2,1,0:T(8,128)(2,1)}) %reduce-scatter.29.cloned.1.call-update) | async-done | bytes 1179664 | tf_op jit(solution)/shard_map/reduce_scatter | solution.py:181
  687.2 2.8 convert_element_type.223
  690.1 85.3 %reduce-scatter.27.cloned.1.call-done = bf16[1,768,768]{2,1,0:T(8,128)(2,1)} async-done(((bf16[1,768,3072]{2,1,0:T(8,128)(2,1)}), bf16[1,768,768]{2,1,0:T(8,128)(2,1)}) %reduce-scatter.27.cloned.1.call-update) | async-done | bytes 1179664 | tf_op jit(solution)/shard_map/reduce_scatter | solution.py:178
  775.4 2.8 convert_element_type.220
  (267 shorter events, 48.2 us)
Async XLA Ops:
  7.2 4.3 copy-start.43
  7.2 43.8 %all-gather.7.cloned.1.call-start = ((), (), s32[]{:S(2)}) async-start(), calls=%async_computation.14 | async-start | bytes 3981312 | tf_op jit(solution)/shard_map/all_gather | solution.py:67
  7.9 69.1 %all-gather.9.cloned.1.call-start = ((), (), s32[]{:S(2)}) async-start(), calls=%async_computation.15 | async-start | bytes 1327104 | tf_op jit(solution)/shard_map/all_gather | solution.py:68
  10.2 11.9 %copy-start.5 = (bf16[394,768]{1,0:T(8,128)(2,1)S(1)}, bf16[394,768]{1,0:T(8,128)(2,1)}, u32[]{:S(2)}) copy-start(bf16[394,768]{1,0:T(8,128)(2,1)} %param.16) | copy-start | bytes 1815556
  11.3 11.8 %copy-start.49 = (bf16[2,96]{1,0:T(2,128)(2,1)S(1)}, bf16[2,96]{1,0:T(2,128)(2,1)}, u32[]{:S(2)}) copy-start(bf16[2,96]{1,0:T(2,128)(2,1)} %param.23) | copy-start | bytes 1156
  11.4 22.2 %copy-start.48 = (bf16[3,96]{1,0:T(4,128)(2,1)S(1)}, bf16[3,96]{1,0:T(4,128)(2,1)}, u32[]{:S(2)}) copy-start(bf16[3,96]{1,0:T(4,128)(2,1)} %param.25) | copy-start | bytes 1732
  11.4 31.6 %copy-start.50 = (bf16[2,96]{1,0:T(2,128)(2,1)S(1)}, bf16[2,96]{1,0:T(2,128)(2,1)}, u32[]{:S(2)}) copy-start(bf16[2,96]{1,0:T(2,128)(2,1)} %param.24) | copy-start | bytes 1156
  16.4 38.3 %copy-start.19 = (s32[394,2]{1,0:T(8,128)}, s32[394,2]{1,0:T(8,128)S(1)}, u32[]{:S(2)}) copy-start(s32[394,2]{1,0:T(8,128)S(1)} %scatter_custom_fusion) | copy-start | bytes 9460
  22.3 32.5 %copy-start.34 = (f32[394]{0:T(512)}, f32[394]{0:T(512)S(1)}, u32[]{:S(2)}) copy-start(f32[394]{0:T(512)S(1)} %broadcast_multiply_fusion.1) | copy-start | bytes 4732
  22.6 32.2 %copy-start.40 = (f32[394]{0:T(512)}, f32[394]{0:T(512)S(1)}, u32[]{:S(2)}) copy-start(f32[394]{0:T(512)S(1)} %fusion.104) | copy-start | bytes 4732
  33.5 21.3 %copy-start.30 = (f32[768]{0:T(1024)}, f32[768]{0:T(1024)S(1)}, u32[]{:S(2)}) copy-start(f32[768]{0:T(1024)S(1)} %get-tuple-element.27) | copy-start | bytes 9220
  33.6 46.2 %copy-start.25 = (f32[768]{0:T(1024)}, f32[768]{0:T(1024)S(1)}, u32[]{:S(2)}) copy-start(f32[768]{0:T(1024)S(1)} %get-tuple-element.26) | copy-start | bytes 9220
  50.9 4.0 copy-start.44
  66.4 5.0 copy-start.7
  68.9 3.4 copy-start.9
  71.4 1.9 copy-start.21
  72.3 2.2 copy-start.2
  77.0 2.4 copy-start.23
  79.4 6.5 copy-start.28
  79.7 6.2 copy-start.38
  79.7 6.2 copy-start.32
  80.7 42.4 %copy-start = (bf16[394,768]{1,0:T(8,128)(2,1)}, bf16[394,768]{1,0:T(8,128)(2,1)S(1)}, u32[]{:S(2)}) copy-start(bf16[394,768]{1,0:T(8,128)(2,1)S(1)} %add_convert_fusion.2) | copy-start | bytes 1815556
  88.8 4.5 copy-start.47
  88.8 28.6 %copy-start.27 = (s32[394,2]{0,1:T(2,128)S(1)}, s32[394,2]{0,1:T(2,128)}, u32[]{:S(2)}) copy-start(s32[394,2]{0,1:T(2,128)} %param.18) | copy-start | bytes 9460
  88.8 28.9 %copy-start.13 = (bf16[394,768]{1,0:T(8,128)(2,1)S(1)}, bf16[394,768]{1,0:T(8,128)(2,1)}, u32[]{:S(2)}) copy-start(bf16[394,768]{1,0:T(8,128)(2,1)} %param.17) | copy-start | bytes 1815556
  88.8 54.6 %all-to-all-start = ((bf16[8,124,768]{2,1,0:T(8,128)(2,1)}), bf16[8,124,768]{2,1,0:T(8,128)(2,1)}, u32[]{:S(2)}, u32[]{:S(2)}) async-start(bf16[8,124,768]{2,1,0:T(8,128)(2,1)} %broadcast_select_fusion.2), calls=%async_computation | async-start | bytes 3145728 | tf_op jit(solution)/shard_map/all_to_all | solution.py:124
  143.4 4.0 copy-start.42
  143.4 4.0 copy-start.46
  143.4 24.9 %all-to-all-start.2 = ((bf16[8,124,768]{2,1,0:T(8,128)(2,1)}), bf16[8,124,768]{2,1,0:T(8,128)(2,1)S(1)}, u32[]{:S(2)}, u32[]{:S(2)}) async-start(bf16[8,124,768]{2,1,0:T(8,128)(2,1)} %reshape.321), calls=%async_computation.2 | async-start | bytes 3145728 | tf_op jit(solution)/shard_map/all_to_all | solution.py:150
  168.3 15.5 %copy-start.11 = (bf16[8,124,768]{2,1,0:T(8,128)(2,1)}, bf16[8,124,768]{2,1,0:T(8,128)(2,1)S(1)}, u32[]{:S(2)}) copy-start(bf16[8,124,768]{2,1,0:T(8,128)(2,1)S(1)} %all-to-all-done.2) | copy-start | bytes 4571140
  183.8 2.6 copy-start.51
  194.9 24.5 %all-to-all-start.3 = ((bf16[8,124,768]{2,1,0:T(8,128)(2,1)}), bf16[8,124,768]{2,1,0:T(8,128)(2,1)S(1)}, u32[]{:S(2)}, u32[]{:S(2)}) async-start(bf16[8,124,768]{2,1,0:T(8,128)(2,1)} %fusion.56), calls=%async_computation.3 | async-start | bytes 3145728 | tf_op jit(solution)/shard_map/all_to_all | solution.py:166
  211.5 12.3 %copy-start.14 = (bf16[394,768]{1,0:T(8,128)(2,1)S(1)}, bf16[394,768]{1,0:T(8,128)(2,1)}, u32[]{:S(2)}) copy-start(bf16[394,768]{1,0:T(8,128)(2,1)} %param.17) | copy-start | bytes 1815556
  219.5 25.3 %all-to-all-start.1 = ((bf16[8,124,768]{2,1,0:T(8,128)(2,1)}), bf16[8,124,768]{2,1,0:T(8,128)(2,1)}, u32[]{:S(2)}, u32[]{:S(2)}) async-start(bf16[8,124,768]{2,1,0:T(8,128)(2,1)} %fusion.61), calls=%async_computation.1 | async-start | bytes 3145728 | tf_op jit(solution)/shard_map/all_to_all | solution.py:137
  223.8 98.2 %reduce-scatter.25.cloned.1.call-start = ((), (), s32[]{:S(2)}) async-start(), calls=%async_computation.17 | async-start | bytes 1327104 | tf_op jit(solution)/shard_map/reduce_scatter | solution.py:267
  251.9 16.1 %copy-start.4 = (f32[394,768]{1,0:T(8,128)S(1)}, f32[394,768]{1,0:T(8,128)}, u32[]{:S(2)}) copy-start(f32[394,768]{1,0:T(8,128)} %copy-done.3) | copy-start | bytes 3631108
  251.9 16.1 %copy-start.26 = (f32[768]{0:T(1024)S(1)}, f32[768]{0:T(1024)}, u32[]{:S(2)}) copy-start(f32[768]{0:T(1024)} %copy-done.25) | copy-start | bytes 9220
  251.9 16.1 %copy-start.29 = (f32[394]{0:T(512)S(1)}, f32[394]{0:T(512)}, u32[]{:S(2)}) copy-start(f32[394]{0:T(512)} %copy-done.28) | copy-start | bytes 4732
  251.9 16.1 %copy-start.33 = (f32[394]{0:T(512)S(1)}, f32[394]{0:T(512)}, u32[]{:S(2)}) copy-start(f32[394]{0:T(512)} %copy-done.32) | copy-start | bytes 4732
  268.1 1.3 copy-start.18
  269.4 1.4 copy-start.15
  269.4 1.4 copy-start.24
  270.7 2.0 copy-start.16
  276.9 87.5 %reduce-scatter.23.cloned.1.call-start = ((), (), s32[]{:S(2)}) async-start(), calls=%async_computation.16 | async-start | bytes 3981312 | tf_op jit(solution)/shard_map/reduce_scatter | solution.py:264
  278.0 9.9 %slice-start = ((s8[4915200]{0:T(1024)(128)(4,1)}), s8[4194304]{0:T(1024)(128)(4,1)S(1)}, s32[]{:S(2)}) async-start(s8[4915200]{0:T(1024)(128)(4,1)} %bitcast.247), calls=%async_computation.27 | async-start | bytes 8388608
  281.9 3.9 copy-start.10
  281.9 5.9 slice-start.1
  293.4 6.6 copy-start.6
  293.4 6.6 copy-start.31
  293.4 6.6 copy-start.35
  293.4 6.6 copy-start.41
  293.4 6.6 copy-start.45
  305.8 1.4 copy-start.12
  305.9 80.3 %reduce-scatter.41.cloned.1.call-start = ((), (), s32[]{:S(2)}) async-start(), calls=%async_computation.25 | async-start | bytes 245760
  308.4 101.9 %reduce-scatter.39.cloned.1.call-start = ((), (), s32[]{:S(2)}) async-start(), calls=%async_computation.24 | async-start | bytes 983040
  310.0 5.0 copy-start.37
  310.1 137.0 %reduce-scatter.35.cloned.1.call-start = ((), (), s32[]{:S(2)}) async-start(), calls=%async_computation.22 | async-start | bytes 221184
  316.4 4.5 copy-start.1
  318.8 165.5 %reduce-scatter.33.cloned.1.call-start = ((), (), s32[]{:S(2)}) async-start(), calls=%async_computation.21 | async-start | bytes 221184
  319.9 201.1 %reduce-scatter.37.cloned.1.call-start = ((), (), s32[]{:S(2)}) async-start(), calls=%async_computation.23 | async-start | bytes 221184
  320.8 237.3 %reduce-scatter.31.cloned.1.call-start = ((), (), s32[]{:S(2)}) async-start(), calls=%async_computation.20 | async-start | bytes 221184
  321.9 278.4 %all-reduce.6.cloned.1.call-start = ((), (), s32[]{:S(2)}) async-start(), calls=%async_computation.26 | async-start | bytes 1179648 | tf_op jit(solution)/shard_map/psum | solution.py:284
  364.4 322.8 %reduce-scatter.29.cloned.1.call-start = ((), (), s32[]{:S(2)}) async-start(), calls=%async_computation.19 | async-start | bytes 5898240 | tf_op jit(solution)/shard_map/reduce_scatter | solution.py:181
  376.7 398.7 %reduce-scatter.27.cloned.1.call-start = ((), (), s32[]{:S(2)}) async-start(), calls=%async_computation.18 | async-start | bytes 5898240 | tf_op jit(solution)/shard_map/reduce_scatter | solution.py:178
  (7 other events, 7.1 us)
Sparse Core Ops, SparseCore 0:
  9.9 36.5 all-gather.6
  48.4 23.9 all-gather.8
  277.0 36.0 reduce-scatter.24
  316.4 47.9 reduce-scatter.22
  366.5 19.5 reduce-scatter.40
  388.9 21.4 reduce-scatter.38
  413.9 33.1 reduce-scatter.34
  450.7 33.5 reduce-scatter.32
  487.3 33.6 reduce-scatter.36
  524.4 33.6 reduce-scatter.30
  560.5 39.7 all-reduce.5
  602.5 84.7 reduce-scatter.28
  689.5 85.7 reduce-scatter.26
where the time goes:
time: 794 us; the launch traced here: 785 us
  waiting for transfers between devices  439 us (55%)
  matrix products  98.8 us (12%)
  local copies, waits for them, and re-layouts  97.9 us (12%)
  blocking collectives  63 us (8%)
  other arithmetic  54.1 us (7%)
  starting transfers between devices  17.2 us (2%)
  between operations  15.3 us (2%)
    unnamed x19, waiting for transfers between devices  168 us
    reduce_scatter x1, waiting for transfers between devices, per_device(): lax.psum_scatter(up_local.astype(jnp.bfloat16), 'dp', scatter_dimension=2...  85.3 us
    reduce_scatter x1, waiting for transfers between devices, per_device(): lax.psum_scatter(down_local.astype(jnp.bfloat16), 'dp', scatter_dimension...  83.3 us
    reduce_scatter x1, waiting for transfers between devices, per_device(): lax.psum_scatter(joint_local.astype(jnp.bfloat16), 'expert', scatter_dime...  42.4 us
    psum x1, waiting for transfers between devices, per_device(): lax.psum(joint_part.astype(jnp.bfloat16), 'dp').astype(jnp.float32)  27.4 us
    unnamed x125, local copies, waits for them, and re-layouts  27.4 us
    all_gather x1, blocking collectives, per_device(): lax.all_gather(router_weight, 'expert', axis=0, tiled=True)  24 us
    reduce_sum x1, other arithmetic, per_device(): gate_grad = jnp.sum(grad_float[:, None, :] * picked, axis=2)  15.9 us
  transfers between devices with their start and end apart: 17, of which 13 were waited for; matrix products, arithmetic and copies ran while one was open for 22% of the time, Pallas kernels for 0%

commit v1 on v0

--- a/solution.py
+++ b/solution.py
@@ -280,8 +280,9 @@
             bias_local.astype(jnp.bfloat16), "expert", scatter_dimension=1, tiled=True
         ).astype(jnp.float32),
     )
+    time_words = lambda local_x: jnp.sum(lax.all_gather(local_x, "dp"), axis=0)
     joint_grad, out_weight_grad, router_grad, gains_grad, shifts_grad, attention_bias_grad = (
-        lax.psum(joint_part.astype(jnp.bfloat16), "dp").astype(jnp.float32),
+        time_words(joint_part.astype(jnp.bfloat16)).astype(jnp.float32),
         lax.psum(out_part.astype(jnp.bfloat16), "dp").astype(jnp.float32),
         lax.psum(router_part.astype(jnp.bfloat16), "dp").astype(jnp.float32),
         lax.psum(gains_part.astype(jnp.bfloat16), "dp").astype(jnp.float32),

time: 794 us -> 830 us (1.045)
  waiting for transfers between devices: 439 us -> 474 us
    all_gather x0 -> x1, waiting for transfers between devices: none -> 40.1 us  [per_device(): time_words = lambda local_x: jnp.sum(lax.all_gather(local_x, 'dp'), axis=0)]
    unnamed x19 -> x20, waiting for transfers between devices: 168 us -> 169 us
  transfers between devices with their start and end apart: 17 -> 18, of which waited for: 13 -> 14; matrix products, arithmetic and copies ran while one was open for 22% -> 21% of each run, Pallas kernels for 0% -> 0%
where the time goes in v1:
time: 830 us; the launch traced here: 821 us
  waiting for transfers between devices  474 us (57%)
  matrix products  98.8 us (12%)
  local copies, waits for them, and re-layouts  97.9 us (12%)
  blocking collectives  63 us (8%)
  other arithmetic  54.9 us (7%)
  starting transfers between devices  17.2 us (2%)
  between operations  15.3 us (2%)
    unnamed x20, waiting for transfers between devices  169 us
    reduce_scatter x1, waiting for transfers between devices, per_device(): lax.psum_scatter(up_local.astype(jnp.bfloat16), 'dp', scatter_dimension=2...  85.2 us
    reduce_scatter x1, waiting for transfers between devices, per_device(): lax.psum_scatter(down_local.astype(jnp.bfloat16), 'dp', scatter_dimension...  83.7 us
    reduce_scatter x1, waiting for transfers between devices, per_device(): lax.psum_scatter(joint_local.astype(jnp.bfloat16), 'expert', scatter_dime...  41.7 us
    all_gather x1, waiting for transfers between devices, per_device(): time_words = lambda local_x: jnp.sum(lax.all_gather(local_x, 'dp'), axis=0)  40.1 us
    unnamed x125, local copies, waits for them, and re-layouts  27.4 us
    all_gather x1, blocking collectives, per_device(): lax.all_gather(router_weight, 'expert', axis=0, tiled=True)  24 us
    psum x1, waiting for transfers between devices, per_device(): lax.psum(out_part.astype(jnp.bfloat16), 'dp').astype(jnp.float32)  22.1 us
  transfers between devices with their start and end apart: 18, of which 14 were waited for; matrix products, arithmetic and copies ran while one was open for 21% of the time, Pallas kernels for 0%

profile of v1, /device:TPU:0, one launch (start us, length us, event | category | flops | bytes accessed | tf_op | source)
XLA Modules:
  0.0 820.8 jit_solution(4943636292951089595)
XLA Ops:
  14.9 1.5 scatter_custom_fusion
  16.8 5.3 scatter_custom_fusion.1
  23.2 10.3 %all-gather.1 = bf16[8,96,2]{1,2,0:T(2,128)(2,1)S(1)} all-gather(bf16[1,96,2]{1,2,0:T(2,128)(2,1)S(1)} %bitcast.276), channel_id=1, replica_groups=mesh['dp'=4,'expert'=8] {'expert'}, dimensions={0}, use_global_device_ids=true | all-gather | bytes 3456 | tf_op jit(solution)/shard_map/all_gather | solution.py:70
  33.6 9.2 %all-gather.3 = bf16[8,96,3]{1,2,0:T(4,128)(2,1)S(1)} all-gather(bf16[1,96,3]{1,2,0:T(4,128)(2,1)S(1)} %bitcast.275), channel_id=1, replica_groups=mesh['dp'=4,'expert'=8] {'expert'}, dimensions={0}, use_global_device_ids=true | all-gather | bytes 5184 | tf_op jit(solution)/shard_map/all_gather | solution.py:72
  42.9 7.8 all-gather.2
  51.0 3.7 fusion.36
  54.8 4.9 reshape.441
  59.8 5.0 fusion.123
  64.7 1.6 copy.210
  66.4 2.5 copy.211
  68.9 2.5 copy.209
  77.1 2.3 fusion.126
  80.7 5.2 gather_fusion.1
  85.9 1.5 gather.20
  88.8 4.4 all-to-all-start
  93.3 24.0 %all-gather.4 = bf16[8,96,8]{1,2,0:T(8,128)(2,1)S(1)} all-gather(bf16[1,96,8]{1,2,0:T(8,128)(2,1)S(1)} %bitcast.274), channel_id=1, replica_groups=mesh['dp'=4,'expert'=8] {'expert'}, dimensions={0}, use_global_device_ids=true | all-gather | bytes 13824 | tf_op jit(solution)/shard_map/all_gather | solution.py:69
  117.7 2.1 mul.253
  119.8 3.3 mul.261
  123.5 8.1 gather_fusion.2
  132.2 8.8 %scatter_custom_fusion.2 = bf16[992,768]{1,0:T(8,128)(2,1)} fusion(s32[788]{0:T(1024)S(1)} %fusion.101, f32[788,768]{1,0:T(8,128)S(1)} %mul.261, f32[788]{0:T(1024)S(1)} %mul.259, bf16[]{:T(256)} %constant.105.clone.1), kind=kCustom, calls=%fused_computation.104 | custom fusion | flops 1210368 | bytes 3960834 | tf_op jit(solution)/shard_map/scatter | solution.py:148
  141.0 2.4 reshape.321
  143.4 3.9 all-to-all-start.2
  147.4 10.0 %fusion.27 = f32[8,124,3072]{2,1,0:T(8,128)} fusion(bf16[8,124,768]{2,1,0:T(8,128)(2,1)} %all-to-all-done, bf16[1,768,3072]{2,1,0:T(8,128)(2,1)} %param.26), kind=kOutput, calls=%fused_computation.46 | convolution fusion | flops 4680843264 | bytes 18432000 | tf_op jit(solution)/shard_map/secd,edf->secf/dot_general | solution.py:127
  157.4 10.9 %all-to-all-done.2 = bf16[8,124,768]{2,1,0:T(8,128)(2,1)S(1)} async-done(((bf16[8,124,768]{2,1,0:T(8,128)(2,1)}), bf16[8,124,768]{2,1,0:T(8,128)(2,1)S(1)}, u32[]{:S(2)}, u32[]{:S(2)}) %all-to-all-start.2) | async-done | bytes 1523744 | tf_op jit(solution)/shard_map/all_to_all | solution.py:150
  168.3 15.5 %fusion.128 = (bf16[3072]{0:T(1024)(128)(2,1)S(1)}, bf16[8,1,124,3072]{3,2,0,1:T(8,128)(2,1)S(1)}) fusion(f32[3072]{0:T(1024)S(1)} %bitcast.266, f32[8,124,3072]{2,1,0:T(8,128)} %fusion.27, bf16[8,124,768]{2,1,0:T(8,128)(2,1)S(1)} %all-to-all-done.2, bf16[1,3072,768]{2,1,0:T(8,128)(2,1)} %param.27), kind=kOutput, calls=%fused_computation.213 | convolution fusion | flops 4747883520 | bytes 24545280 | tf_op jit(solution)/shard_map/secd,efd->secf/dot_general | solution.py:158
  183.8 2.6 copy-done.51
  186.4 8.5 %fusion.56 = bf16[8,124,768]{2,1,0:T(8,128)(2,1)} fusion(bf16[1,768,3072]{2,1,0:T(8,128)(2,1)} %param.26, bf16[8,1,124,3072]{3,2,0,1:T(8,128)(2,1)S(1)} %get-tuple-element.61), kind=kOutput, calls=%fused_computation.78 | convolution fusion | flops 4681605120 | bytes 12337152 | tf_op jit(solution)/shard_map/secf,edf->secd/dot_general | solution.py:163
  194.9 3.6 all-to-all-start.3
  198.5 13.0 %fusion.61 = bf16[8,124,768]{2,1,0:T(8,128)(2,1)} fusion(f32[768]{0:T(1024)S(1)} %convert_reduce_fusion.3, bf16[1,3072,768]{2,1,0:T(8,128)(2,1)} %param.27, f32[8,124,3072]{2,1,0:T(8,128)} %fusion.27, f32[3072]{0:T(1024)S(1)} %bitcast.267), kind=kOutput, calls=%fused_computation.83 | convolution fusion | flops 4712841216 | bytes 18447360 | tf_op jit(solution)/shard_map/secf,efd->secd/dot_general | solution.py:133
  211.5 8.0 all-to-all-done.3
  219.5 4.3 all-to-all-start.1
  226.0 3.7 gather_fusion.4
  229.7 1.9 reshape.424
  231.6 13.2 %all-to-all-done.1 = bf16[8,124,768]{2,1,0:T(8,128)(2,1)} async-done(((bf16[8,124,768]{2,1,0:T(8,128)(2,1)}), bf16[8,124,768]{2,1,0:T(8,128)(2,1)}, u32[]{:S(2)}, u32[]{:S(2)}) %all-to-all-start.1) | async-done | bytes 1523744 | tf_op jit(solution)/shard_map/all_to_all | solution.py:137
  244.8 1.5 reshape.320
  246.3 3.7 gather_fusion.3
  250.0 1.9 reshape.420
  251.9 15.9 %fusion.47 = (f32[394,2]{1,0:T(8,128)S(1)}, f32[394,768]{1,0:T(8,128)}, f32[394,768]{1,0:T(8,128)S(1)}) fusion(f32[394,768]{1,0:T(8,128)} %convert_element_type.197, bf16[394,2,768]{2,1,0:T(2,128)(2,1)} %reshape.420, pred[394,2]{1,0:T(8,128)(4,1)S(1)} %compare_and_fusion, f32[394,2]{1,0:T(8,128)S(1)} %copy.171, bf16[394,2,768]{2,1,0:T(2,128)(2,1)} %reshape.424), kind=kLoop, calls=%fused_computation.65 | loop fusion | flops 4840684 | bytes 6058932 | tf_op jit(solution)/shard_map/reduce_sum | solution.py:143
  270.8 1.9 convolution_convert_fusion.1
  272.7 2.0 convolution_convert_fusion.2
  278.0 3.9 multiply_reduce_fusion
  281.9 3.8 multiply_convert_fusion.1
  289.5 3.9 copy.184
  293.4 6.6 convert_element_type.208
  300.0 5.8 convolution_convert_fusion
  310.1 5.0 fusion.120
  316.4 1.5 fusion.119
  322.7 41.7 %reduce-scatter.23.cloned.1.call-done = bf16[96,2304]{1,0:T(8,128)(2,1)} async-done(((bf16[768,2304]{1,0:T(8,128)(2,1)}), bf16[96,2304]{1,0:T(8,128)(2,1)}) %reduce-scatter.23.cloned.1.call-update) | async-done | bytes 442384 | tf_op jit(solution)/shard_map/reduce_scatter | solution.py:264
  364.5 12.2 %fusion.32 = bf16[1,3072,768]{2,1,0:T(8,128)(2,1)} fusion(bf16[8,124,768]{2,1,0:T(8,128)(2,1)S(1)} %copy-done.12, f32[8,124,3072]{2,1,0:T(8,128)} %fusion.27, f32[3072]{0:T(1024)S(1)} %bitcast.268), kind=kOutput, calls=%fused_computation.49 | convolution fusion | flops 4713676800 | bytes 18444288 | tf_op jit(solution)/shard_map/secf,secd->efd/dot_general | solution.py:172
  376.7 9.1 %fusion.29 = bf16[1,768,3072]{2,1,0:T(8,128)(2,1)} fusion(bf16[8,124,768]{2,1,0:T(8,128)(2,1)} %all-to-all-done, bf16[8,1,124,3072]{3,2,0,1:T(8,128)(2,1)} %copy-done.51), kind=kOutput, calls=%fused_computation.48 | convolution fusion | flops 4683202560 | bytes 12337152 | tf_op jit(solution)/shard_map/secd,secf->edf/dot_general | solution.py:169
  387.6 22.7 %reduce-scatter.39.cloned.1.call-done = bf16[768,1]{1,0:T(8,128)(2,1)} async-done(((bf16[3072,1]{1,0:T(8,128)(2,1)}), bf16[768,1]{1,0:T(8,128)(2,1)}) %reduce-scatter.39.cloned.1.call-update) | async-done | bytes 1552
  412.0 35.1 %reduce-scatter.35.cloned.1.call-done = bf16[96,2]{1,0:T(8,128)(2,1)} async-done(((bf16[768,2]{1,0:T(8,128)(2,1)}), bf16[96,2]{1,0:T(8,128)(2,1)}) %reduce-scatter.35.cloned.1.call-update) | async-done | bytes 400
  447.9 36.4 %reduce-scatter.33.cloned.1.call-done = bf16[96,2]{1,0:T(8,128)(2,1)} async-done(((bf16[768,2]{1,0:T(8,128)(2,1)}), bf16[96,2]{1,0:T(8,128)(2,1)}) %reduce-scatter.33.cloned.1.call-update) | async-done | bytes 400
  485.1 35.9 %reduce-scatter.37.cloned.1.call-done = bf16[96,3]{1,0:T(8,128)(2,1)} async-done(((bf16[768,3]{1,0:T(8,128)(2,1)}), bf16[96,3]{1,0:T(8,128)(2,1)}) %reduce-scatter.37.cloned.1.call-update) | async-done | bytes 592
  521.8 36.3 %reduce-scatter.31.cloned.1.call-done = bf16[96,8]{1,0:T(8,128)(2,1)} async-done(((bf16[768,8]{1,0:T(8,128)(2,1)}), bf16[96,8]{1,0:T(8,128)(2,1)}) %reduce-scatter.31.cloned.1.call-update) | async-done | bytes 1552
  558.9 11.7 %all-reduce.2 = (bf16[96,8]{0,1:T(8,128)(2,1)S(1)}, bf16[2,96]{1,0:T(2,128)(2,1)S(1)}, bf16[2,96]{1,0:T(2,128)(2,1)S(1)}, bf16[3,96]{1,0:T(4,128)(2,1)S(1)}) all-reduce(bf16[96,8]{0,1:T(8,128)(2,1)S(1)} %copy.194, bf16[2,96]{1,0:T(2,128)(2,1)S(1)} %copy.196, ...), channel_id=1, replica_groups=mesh['dp'=4,'expert'=8] {'dp'}, use_global_device_ids=true, to_apply=%region_33.35 | all-reduce | flops 1440 | bytes 5760 | tf_op jit(solution)/shard_map/psum | solution.py:287
  572.9 22.1 %all-reduce.5.cloned.1.call-done = bf16[96,768]{1,0:T(8,128)(2,1)} async-done(((bf16[96,768]{1,0:T(8,128)(2,1)}), bf16[96,768]{1,0:T(8,128)(2,1)}) %all-reduce.5.cloned.1.call-update) | async-done | bytes 147472 | tf_op jit(solution)/shard_map/psum | solution.py:286
  595.0 1.6 convert_element_type.213
  596.6 40.1 %all-gather.13.cloned.1.call-done = bf16[384,2304]{1,0:T(8,128)(2,1)} async-done(((bf16[96,2304]{1,0:T(8,128)(2,1)}), bf16[384,2304]{1,0:T(8,128)(2,1)}) %all-gather.13.cloned.1.call-update) | async-done | bytes 1769488 | tf_op jit(solution)/shard_map/all_gather | solution.py:283
  636.7 1.8 reduce_sum.316
  639.4 83.7 %reduce-scatter.29.cloned.1.call-done = bf16[1,768,768]{2,1,0:T(8,128)(2,1)} async-done(((bf16[1,3072,768]{2,1,0:T(8,128)(2,1)}), bf16[1,768,768]{2,1,0:T(8,128)(2,1)}) %reduce-scatter.29.cloned.1.call-update) | async-done | bytes 1179664 | tf_op jit(solution)/shard_map/reduce_scatter | solution.py:181
  723.1 2.8 convert_element_type.225
  726.0 85.2 %reduce-scatter.27.cloned.1.call-done = bf16[1,768,768]{2,1,0:T(8,128)(2,1)} async-done(((bf16[1,768,3072]{2,1,0:T(8,128)(2,1)}), bf16[1,768,768]{2,1,0:T(8,128)(2,1)}) %reduce-scatter.27.cloned.1.call-update) | async-done | bytes 1179664 | tf_op jit(solution)/shard_map/reduce_scatter | solution.py:178
  811.1 2.8 convert_element_type.222
  (271 shorter events, 51.2 us)
Async XLA Ops:
  7.2 4.3 copy-start.43
  7.2 43.8 %all-gather.9.cloned.1.call-start = ((), (), s32[]{:S(2)}) async-start(), calls=%async_computation.14 | async-start | bytes 3981312 | tf_op jit(solution)/shard_map/all_gather | solution.py:67
  7.9 69.1 %all-gather.11.cloned.1.call-start = ((), (), s32[]{:S(2)}) async-start(), calls=%async_computation.15 | async-start | bytes 1327104 | tf_op jit(solution)/shard_map/all_gather | solution.py:68
  10.2 11.9 %copy-start.5 = (bf16[394,768]{1,0:T(8,128)(2,1)S(1)}, bf16[394,768]{1,0:T(8,128)(2,1)}, u32[]{:S(2)}) copy-start(bf16[394,768]{1,0:T(8,128)(2,1)} %param.16) | copy-start | bytes 1815556
  11.3 11.8 %copy-start.49 = (bf16[2,96]{1,0:T(2,128)(2,1)S(1)}, bf16[2,96]{1,0:T(2,128)(2,1)}, u32[]{:S(2)}) copy-start(bf16[2,96]{1,0:T(2,128)(2,1)} %param.23) | copy-start | bytes 1156
  11.4 22.2 %copy-start.48 = (bf16[3,96]{1,0:T(4,128)(2,1)S(1)}, bf16[3,96]{1,0:T(4,128)(2,1)}, u32[]{:S(2)}) copy-start(bf16[3,96]{1,0:T(4,128)(2,1)} %param.25) | copy-start | bytes 1732
  11.4 31.6 %copy-start.50 = (bf16[2,96]{1,0:T(2,128)(2,1)S(1)}, bf16[2,96]{1,0:T(2,128)(2,1)}, u32[]{:S(2)}) copy-start(bf16[2,96]{1,0:T(2,128)(2,1)} %param.24) | copy-start | bytes 1156
  16.4 38.3 %copy-start.19 = (s32[394,2]{1,0:T(8,128)}, s32[394,2]{1,0:T(8,128)S(1)}, u32[]{:S(2)}) copy-start(s32[394,2]{1,0:T(8,128)S(1)} %scatter_custom_fusion) | copy-start | bytes 9460
  22.3 32.5 %copy-start.34 = (f32[394]{0:T(512)}, f32[394]{0:T(512)S(1)}, u32[]{:S(2)}) copy-start(f32[394]{0:T(512)S(1)} %broadcast_multiply_fusion.1) | copy-start | bytes 4732
  22.6 32.2 %copy-start.40 = (f32[394]{0:T(512)}, f32[394]{0:T(512)S(1)}, u32[]{:S(2)}) copy-start(f32[394]{0:T(512)S(1)} %fusion.104) | copy-start | bytes 4732
  33.5 21.3 %copy-start.30 = (f32[768]{0:T(1024)}, f32[768]{0:T(1024)S(1)}, u32[]{:S(2)}) copy-start(f32[768]{0:T(1024)S(1)} %get-tuple-element.27) | copy-start | bytes 9220
  33.6 46.2 %copy-start.25 = (f32[768]{0:T(1024)}, f32[768]{0:T(1024)S(1)}, u32[]{:S(2)}) copy-start(f32[768]{0:T(1024)S(1)} %get-tuple-element.26) | copy-start | bytes 9220
  50.9 4.0 copy-start.44
  66.4 5.0 copy-start.7
  68.9 3.4 copy-start.9
  71.4 1.9 copy-start.21
  72.3 2.2 copy-start.2
  77.0 2.4 copy-start.23
  79.4 6.5 copy-start.28
  79.7 6.2 copy-start.38
  79.7 6.2 copy-start.32
  80.7 42.4 %copy-start = (bf16[394,768]{1,0:T(8,128)(2,1)}, bf16[394,768]{1,0:T(8,128)(2,1)S(1)}, u32[]{:S(2)}) copy-start(bf16[394,768]{1,0:T(8,128)(2,1)S(1)} %add_convert_fusion.2) | copy-start | bytes 1815556
  88.8 4.5 copy-start.47
  88.8 28.6 %copy-start.27 = (s32[394,2]{0,1:T(2,128)S(1)}, s32[394,2]{0,1:T(2,128)}, u32[]{:S(2)}) copy-start(s32[394,2]{0,1:T(2,128)} %param.18) | copy-start | bytes 9460
  88.8 28.9 %copy-start.13 = (bf16[394,768]{1,0:T(8,128)(2,1)S(1)}, bf16[394,768]{1,0:T(8,128)(2,1)}, u32[]{:S(2)}) copy-start(bf16[394,768]{1,0:T(8,128)(2,1)} %param.17) | copy-start | bytes 1815556
  88.8 54.6 %all-to-all-start = ((bf16[8,124,768]{2,1,0:T(8,128)(2,1)}), bf16[8,124,768]{2,1,0:T(8,128)(2,1)}, u32[]{:S(2)}, u32[]{:S(2)}) async-start(bf16[8,124,768]{2,1,0:T(8,128)(2,1)} %broadcast_select_fusion.2), calls=%async_computation | async-start | bytes 3145728 | tf_op jit(solution)/shard_map/all_to_all | solution.py:124
  143.4 4.0 copy-start.42
  143.4 4.0 copy-start.46
  143.4 24.9 %all-to-all-start.2 = ((bf16[8,124,768]{2,1,0:T(8,128)(2,1)}), bf16[8,124,768]{2,1,0:T(8,128)(2,1)S(1)}, u32[]{:S(2)}, u32[]{:S(2)}) async-start(bf16[8,124,768]{2,1,0:T(8,128)(2,1)} %reshape.321), calls=%async_computation.2 | async-start | bytes 3145728 | tf_op jit(solution)/shard_map/all_to_all | solution.py:150
  168.3 15.5 %copy-start.11 = (bf16[8,124,768]{2,1,0:T(8,128)(2,1)}, bf16[8,124,768]{2,1,0:T(8,128)(2,1)S(1)}, u32[]{:S(2)}) copy-start(bf16[8,124,768]{2,1,0:T(8,128)(2,1)S(1)} %all-to-all-done.2) | copy-start | bytes 4571140
  183.8 2.6 copy-start.51
  194.9 24.5 %all-to-all-start.3 = ((bf16[8,124,768]{2,1,0:T(8,128)(2,1)}), bf16[8,124,768]{2,1,0:T(8,128)(2,1)S(1)}, u32[]{:S(2)}, u32[]{:S(2)}) async-start(bf16[8,124,768]{2,1,0:T(8,128)(2,1)} %fusion.56), calls=%async_computation.3 | async-start | bytes 3145728 | tf_op jit(solution)/shard_map/all_to_all | solution.py:166
  211.5 12.3 %copy-start.14 = (bf16[394,768]{1,0:T(8,128)(2,1)S(1)}, bf16[394,768]{1,0:T(8,128)(2,1)}, u32[]{:S(2)}) copy-start(bf16[394,768]{1,0:T(8,128)(2,1)} %param.17) | copy-start | bytes 1815556
  219.5 25.3 %all-to-all-start.1 = ((bf16[8,124,768]{2,1,0:T(8,128)(2,1)}), bf16[8,124,768]{2,1,0:T(8,128)(2,1)}, u32[]{:S(2)}, u32[]{:S(2)}) async-start(bf16[8,124,768]{2,1,0:T(8,128)(2,1)} %fusion.61), calls=%async_computation.1 | async-start | bytes 3145728 | tf_op jit(solution)/shard_map/all_to_all | solution.py:137
  223.8 98.2 %reduce-scatter.25.cloned.1.call-start = ((), (), s32[]{:S(2)}) async-start(), calls=%async_computation.17 | async-start | bytes 1327104 | tf_op jit(solution)/shard_map/reduce_scatter | solution.py:267
  251.9 16.1 %copy-start.4 = (f32[394,768]{1,0:T(8,128)S(1)}, f32[394,768]{1,0:T(8,128)}, u32[]{:S(2)}) copy-start(f32[394,768]{1,0:T(8,128)} %copy-done.3) | copy-start | bytes 3631108
  251.9 16.1 %copy-start.26 = (f32[768]{0:T(1024)S(1)}, f32[768]{0:T(1024)}, u32[]{:S(2)}) copy-start(f32[768]{0:T(1024)} %copy-done.25) | copy-start | bytes 9220
  251.9 16.1 %copy-start.29 = (f32[394]{0:T(512)S(1)}, f32[394]{0:T(512)}, u32[]{:S(2)}) copy-start(f32[394]{0:T(512)} %copy-done.28) | copy-start | bytes 4732
  251.9 16.1 %copy-start.33 = (f32[394]{0:T(512)S(1)}, f32[394]{0:T(512)}, u32[]{:S(2)}) copy-start(f32[394]{0:T(512)} %copy-done.32) | copy-start | bytes 4732
  269.4 1.4 copy-start.15
  269.4 1.4 copy-start.24
  270.7 2.0 copy-start.16
  276.9 87.5 %reduce-scatter.23.cloned.1.call-start = ((), (), s32[]{:S(2)}) async-start(), calls=%async_computation.16 | async-start | bytes 3981312 | tf_op jit(solution)/shard_map/reduce_scatter | solution.py:264
  278.0 9.9 %slice-start = ((s8[4915200]{0:T(1024)(128)(4,1)}), s8[4194304]{0:T(1024)(128)(4,1)S(1)}, s32[]{:S(2)}) async-start(s8[4915200]{0:T(1024)(128)(4,1)} %bitcast.248), calls=%async_computation.28 | async-start | bytes 8388608
  281.9 3.9 copy-start.10
  281.9 5.9 slice-start.1
  293.4 6.6 copy-start.6
  293.4 6.6 copy-start.31
  293.4 6.6 copy-start.35
  293.4 6.6 copy-start.41
  293.4 6.6 copy-start.45
  305.8 1.4 copy-start.12
  305.9 80.3 %reduce-scatter.41.cloned.1.call-start = ((), (), s32[]{:S(2)}) async-start(), calls=%async_computation.27 | async-start | bytes 245760
  308.4 101.9 %reduce-scatter.39.cloned.1.call-start = ((), (), s32[]{:S(2)}) async-start(), calls=%async_computation.26 | async-start | bytes 983040
  310.0 5.0 copy-start.37
  310.1 137.0 %reduce-scatter.35.cloned.1.call-start = ((), (), s32[]{:S(2)}) async-start(), calls=%async_computation.24 | async-start | bytes 221184
  316.4 4.5 copy-start.1
  318.8 165.5 %reduce-scatter.33.cloned.1.call-start = ((), (), s32[]{:S(2)}) async-start(), calls=%async_computation.23 | async-start | bytes 221184
  319.9 201.1 %reduce-scatter.37.cloned.1.call-start = ((), (), s32[]{:S(2)}) async-start(), calls=%async_computation.25 | async-start | bytes 221184
  320.8 237.3 %reduce-scatter.31.cloned.1.call-start = ((), (), s32[]{:S(2)}) async-start(), calls=%async_computation.22 | async-start | bytes 221184
  321.9 273.0 %all-reduce.5.cloned.1.call-start = ((), (), s32[]{:S(2)}) async-start(), calls=%async_computation.18 | async-start | bytes 294912 | tf_op jit(solution)/shard_map/psum | solution.py:286
  322.7 314.0 %all-gather.13.cloned.1.call-start = ((), (), s32[]{:S(2)}) async-start(), calls=%async_computation.21 | async-start | bytes 2211840 | tf_op jit(solution)/shard_map/all_gather | solution.py:283
  364.4 358.7 %reduce-scatter.29.cloned.1.call-start = ((), (), s32[]{:S(2)}) async-start(), calls=%async_computation.20 | async-start | bytes 5898240 | tf_op jit(solution)/shard_map/reduce_scatter | solution.py:181
  376.7 434.5 %reduce-scatter.27.cloned.1.call-start = ((), (), s32[]{:S(2)}) async-start(), calls=%async_computation.19 | async-start | bytes 5898240 | tf_op jit(solution)/shard_map/reduce_scatter | solution.py:178
  (8 other events, 8.4 us)
Sparse Core Ops, SparseCore 0:
  9.9 36.5 all-gather.8
  48.4 23.9 all-gather.10
  277.0 36.0 reduce-scatter.24
  316.4 47.9 reduce-scatter.22
  366.5 19.5 reduce-scatter.40
  388.9 21.4 reduce-scatter.38
  413.9 33.1 reduce-scatter.34
  450.7 33.5 reduce-scatter.32
  487.3 33.6 reduce-scatter.36
  524.4 33.6 reduce-scatter.30
  560.4 34.4 all-reduce.4
  596.4 40.2 all-gather.12
  639.0 84.1 reduce-scatter.28
  725.3 85.7 reduce-scatter.26
